TPU v7x, 32 devices: a whole 2x2x4 slice. The times are simulated.
32 devices in a mesh: row: 4 (over y, x), col: 8 (over z, core).
Axes of the slice: x: 2, y: 2, z: 4, core: 2. Of those that a mesh axis runs over, the one named last changes fastest.
Arguments:
- noise: float32 [2048, 3072], P('row', 'col'), may hold values from -30 to 30
- images: float32 [6144, 3072], P('col', 'row'), may hold values from -6 to 6
- time_index: int32 [2048], P('row'), may hold values from 0 to 999
- w_in: float32 [3072, 3072], P(None, 'col'), may hold values from -0.109375 to 0.109375
- time_gain: float32 [3072], P('col'), may hold values from -5 to 5
- w_out: float32 [3072, 3072], P('col'), may hold values from -0.109375 to 0.109375
Outputs:
- targets: float32 [2048, 3072], P('row', 'col')
- row_pot: float32 [2048], P('row')
- col_pot: float32 [6144], P('col')
- grad_in: float32 [3072, 3072], P('row', 'col')
- grad_time: float32 [3072], P('col')
- grad_out: float32 [3072, 3072], P('col', 'row')
- mse: float32 [], replicated
All inputs are finite; a program needn't handle non-finite values.
Results may differ from a plain program's by a relative error of at most 0.0003.
Values sent between devices are 32-bit elements; how exact they have to be, the bound alone decides.
A program may use at most 128 MiB of HBM per device.

v0:
```python
import jax
import jax.numpy as jnp
from jax import lax
from jax.sharding import PartitionSpec as P

ITERS = 2
TIMES = 1000
EPSILON = 0.01


def merged(array, axis, combine):
    everything = jax.tree.map(lambda part: lax.all_gather(part, axis), array)
    first = jax.tree.map(lambda part: part[0], everything)

    def hop(k, so_far):
        return combine(so_far, jax.tree.map(lambda part: part[k], everything))

    return lax.fori_loop(1, lax.axis_size(axis), hop, first)


def joined(left_pair, right_pair):
    peak = jnp.maximum(left_pair[0], right_pair[0])
    total = left_pair[1] * jnp.exp(left_pair[0] - peak) + right_pair[1] * jnp.exp(
        right_pair[0] - peak
    )
    return (peak, total)


def over_images(logits):
    local_peak = jnp.max(logits, axis=1)
    local_total = jnp.sum(jnp.exp(logits - local_peak[:, None]), axis=1)
    peak, total = merged((local_peak, local_total), "col", joined)
    return (peak, total)


def over_noise(logits):
    local_peak = jnp.max(logits, axis=0)
    local_total = jnp.sum(jnp.exp(logits - local_peak[None, :]), axis=0)
    peak, total = merged((local_peak, local_total), "row", joined)
    return (peak, total)


def body(noise, images, time_index, w_in, time_gain, w_out):
    highest = lax.Precision.HIGHEST
    full_noise = lax.all_gather(noise, "col", axis=1, tiled=True)
    full_images = lax.all_gather(images, "row", axis=1, tiled=True)
    width = full_noise.shape[1]
    noise_count = full_noise.shape[0] * lax.axis_size("row")
    image_count = full_images.shape[0] * lax.axis_size("col")
    noise_norms = jnp.sum(full_noise * full_noise, axis=1)
    image_norms = jnp.sum(full_images * full_images, axis=1)
    cross = lax.dot_general(
        full_noise,
        full_images,
        (((1,), (1,)), ((), ())),
        precision=highest,
        preferred_element_type=jnp.float32,
    )
    scaled = (noise_norms[:, None] + image_norms[None, :] - 2.0 * cross) / (width * EPSILON)
    col_pot = jnp.zeros((full_images.shape[0],), jnp.float32)
    row_pot = jnp.zeros((full_noise.shape[0],), jnp.float32)
    for iteration in range(ITERS):
        peak, total = over_images(col_pot[None, :] - scaled)
        row_pot = jnp.log(jnp.float32(image_count)) - (jnp.log(total) + peak)
        peak, total = over_noise(row_pot[:, None] - scaled)
        col_pot = jnp.log(jnp.float32(noise_count)) - (jnp.log(total) + peak)
    logits = col_pot[None, :] - scaled
    peak, total = over_images(logits)
    weights = jnp.exp(logits - (jnp.log(total) + peak)[:, None])
    partial_value = jnp.dot(
        weights, full_images, precision=highest, preferred_element_type=jnp.float32
    )
    slice_width = noise.shape[1]
    slice_start = lax.axis_index("col") * slice_width
    whole_targets = lax.psum(partial_value, "col")
    targets = lax.dynamic_slice_in_dim(whole_targets, slice_start, slice_width, 1)
    fraction = (time_index.astype(jnp.float32) + 0.5) / TIMES
    mixed = (1.0 - fraction)[:, None] * full_noise + fraction[:, None] * whole_targets
    velocity = whole_targets - full_noise
    pre = (
        jnp.dot(mixed, w_in, precision=highest, preferred_element_type=jnp.float32)
        + fraction[:, None] * time_gain[None, :]
    )
    sigma = jax.nn.sigmoid(pre)
    hidden = pre * sigma
    part_out = jnp.dot(hidden, w_out, precision=highest, preferred_element_type=jnp.float32)
    out = lax.psum(part_out, "col")
    diff = out - velocity
    squared = jnp.sum(diff * diff)
    slope = diff / jnp.sqrt(jnp.float32(noise_count))
    local_out = lax.dot_general(
        hidden,
        slope,
        (((0,), (0,)), ((), ())),
        precision=highest,
        preferred_element_type=jnp.float32,
    )
    back = lax.dot_general(
        slope,
        w_out,
        (((1,), (1,)), ((), ())),
        precision=highest,
        preferred_element_type=jnp.float32,
    )
    dpre = back * sigma * (1.0 + pre * (1.0 - sigma))
    local_in = lax.dot_general(
        mixed, dpre, (((0,), (0,)), ((), ())), precision=highest, preferred_element_type=jnp.float32
    )
    local_time = jnp.sum(fraction[:, None] * dpre, axis=0)
    grad_in, grad_out = (
        lax.psum_scatter(local_in, "row", scatter_dimension=0, tiled=True),
        lax.psum_scatter(local_out, "row", scatter_dimension=1, tiled=True),
    )
    grad_time, squared_all = lax.psum((local_time, squared), "row")
    mse = squared_all / (noise_count * width)
    return (targets, row_pot, col_pot, grad_in, grad_time, grad_out, mse)


def solution(mesh):
    placed = (P("row", "col"), P("col", "row"), P("row"), P(None, "col"), P("col"), P("col", None))
    return jax.shard_map(
        body,
        mesh=mesh,
        in_specs=placed,
        out_specs=(
            P("row", "col"),
            P("row"),
            P("col"),
            P("row", "col"),
            P("col"),
            P("col", "row"),
            P(),
        ),
        check_vma=False,
    )
```

profile of v0, /device:TPU:0, one launch (start us, length us, event | category | flops | bytes accessed | tf_op | source)
XLA Modules:
  0.0 786.1 jit_solution(18099109052659360453)
XLA Ops:
  8.7 68.3 %all-gather.23.cloned.1.call-done = f32[512,3072]{1,0:T(8,128)} async-done(((f32[512,384]{1,0:T(8,128)}), f32[512,3072]{1,0:T(8,128)}) %all-gather.23.cloned.1.call-update) | async-done | bytes 6291472 | tf_op jit(solution)/shard_map/all_gather | solution.py:45
  80.3 93.5 %all-gather.25.cloned.1.call-done = f32[768,3072]{1,0:T(8,128)} async-done(((f32[768,768]{1,0:T(8,128)}), f32[768,3072]{1,0:T(8,128)}) %all-gather.25.cloned.1.call-update) | async-done | bytes 9437200 | tf_op jit(solution)/shard_map/all_gather | solution.py:46
  179.2 18.3 %subtract_reduce_fusion.3 = (f32[512]{0:T(512)S(1)}, f32[512,768]{1,0:T(8,128)S(1)}) fusion(f32[512,3072]{1,0:T(8,128)S(1)} %copy-done, f32[768,3072]{1,0:T(8,128)} %all-gather.25.cloned.1.call-done, f32[768]{0:T(1024)S(1)} %multiply_reduce_fusion, f32[512]{0:T(512)S(1)} %multiply_reduce_fusion.2), kind=kOutput, calls=%fused_computation.38 | convolution fusion | flops 14497873920 | bytes 17308672 | tf_op jit(solution)/shard_map/dot_general | solution.py:52
  197.9 12.8 %all-gather.11 = f32[8,1,512]{2,1,0:T(1,128)S(1)} all-gather(f32[1,1,512]{2,1,0:T(1,128)S(1)} %bitcast.95), channel_id=3, replica_groups=mesh['row'=4,'col'=8] {'col'}, dimensions={0}, use_global_device_ids=true | all-gather | bytes 18432 | tf_op jit(solution)/shard_map/all_gather | solution.py:12
  210.8 12.8 %all-gather.10 = f32[8,1,512]{2,1,0:T(1,128)S(1)} all-gather(f32[1,1,512]{2,1,0:T(1,128)S(1)} %bitcast.93), channel_id=2, replica_groups=mesh['row'=4,'col'=8] {'col'}, dimensions={0}, use_global_device_ids=true | all-gather | bytes 18432 | tf_op jit(solution)/shard_map/all_gather | solution.py:12
  224.5 8.1 %all-gather.13 = f32[4,1,768]{2,1,0:T(1,128)S(1)} all-gather(f32[1,1,768]{2,1,0:T(1,128)S(1)} %reshape.65), channel_id=5, replica_groups=mesh['row'=4,'col'=8] {'row'}, dimensions={0}, use_global_device_ids=true | all-gather | bytes 15360 | tf_op jit(solution)/shard_map/all_gather | solution.py:12
  240.7 12.8 %all-gather.15 = f32[8,1,512]{2,1,0:T(1,128)S(1)} all-gather(f32[1,1,512]{2,1,0:T(1,128)S(1)} %bitcast.94), channel_id=7, replica_groups=mesh['row'=4,'col'=8] {'col'}, dimensions={0}, use_global_device_ids=true | all-gather | bytes 18432 | tf_op jit(solution)/shard_map/all_gather | solution.py:12
  253.5 12.8 %all-gather.14 = f32[8,1,512]{2,1,0:T(1,128)S(1)} all-gather(f32[1,1,512]{2,1,0:T(1,128)S(1)} %bitcast.91), channel_id=6, replica_groups=mesh['row'=4,'col'=8] {'col'}, dimensions={0}, use_global_device_ids=true | all-gather | bytes 18432 | tf_op jit(solution)/shard_map/all_gather | solution.py:12
  267.2 8.1 %all-gather.17 = f32[4,1,768]{2,1,0:T(1,128)S(1)} all-gather(f32[1,1,768]{2,1,0:T(1,128)S(1)} %reshape.73), channel_id=9, replica_groups=mesh['row'=4,'col'=8] {'row'}, dimensions={0}, use_global_device_ids=true | all-gather | bytes 15360 | tf_op jit(solution)/shard_map/all_gather | solution.py:12
  275.4 18.3 %all-gather.16 = f32[4,1,768]{2,1,0:T(1,128)S(1)} all-gather(f32[1,1,768]{2,1,0:T(1,128)S(1)} %reshape.71), channel_id=8, replica_groups=mesh['row'=4,'col'=8] {'row'}, dimensions={0}, use_global_device_ids=true | all-gather | bytes 15360 | tf_op jit(solution)/shard_map/all_gather | solution.py:12
  294.6 12.8 %all-gather.19 = f32[8,1,512]{2,1,0:T(1,128)S(1)} all-gather(f32[1,1,512]{2,1,0:T(1,128)S(1)} %bitcast.96), channel_id=11, replica_groups=mesh['row'=4,'col'=8] {'col'}, dimensions={0}, use_global_device_ids=true | all-gather | bytes 18432 | tf_op jit(solution)/shard_map/all_gather | solution.py:12
  307.3 12.8 %all-gather.18 = f32[8,1,512]{2,1,0:T(1,128)S(1)} all-gather(f32[1,1,512]{2,1,0:T(1,128)S(1)} %bitcast.92), channel_id=10, replica_groups=mesh['row'=4,'col'=8] {'col'}, dimensions={0}, use_global_device_ids=true | all-gather | bytes 18432 | tf_op jit(solution)/shard_map/all_gather | solution.py:12
  320.5 19.3 %fusion.6 = f32[512,3072]{1,0:T(8,128)} fusion(f32[768,3072]{1,0:T(8,128)} %all-gather.25.cloned.1.call-done, f32[512,768]{1,0:T(8,128)S(1)} %get-tuple-element.759, f32[512]{0:T(512)S(1)} %log_add_fusion, f32[768]{0:T(1024)S(1)} %add_subtract_fusion), kind=kOutput, calls=%fused_computation.26 | convolution fusion | flops 14496301056 | bytes 17306624 | tf_op jit(solution)/shard_map/dot_general | solution.py:70
  340.4 133.1 %all-reduce.4.cloned.1.call-done = f32[512,3072]{1,0:T(8,128)} async-done(((f32[512,3072]{1,0:T(8,128)}), f32[512,3072]{1,0:T(8,128)}) %all-reduce.4.cloned.1.call-update) | async-done | bytes 6291472 | tf_op jit(solution)/shard_map/psum | solution.py:75
  473.6 14.6 %convolution_add_fusion = f32[512,384]{1,0:T(8,128)S(1)} fusion(f32[3072,384]{1,0:T(8,128)} %param.19, f32[384]{0:T(512)S(1)} %copy-done.7, f32[512]{0:T(512)S(1)} %get-tuple-element.757, f32[512,3072]{1,0:T(8,128)} %all-reduce.4.cloned.1.call-done, f32[512,3072]{1,0:T(8,128)} %all-gather.23.cloned.1.call-done, f32[512]{0:T(512)S(1)} %get-tuple-element.756), kind=kOutput, calls=%fused_computation.43 | convolution fusion | flops 7252869120 | bytes 18093568 | tf_op jit(solution)/shard_map/dot_general | solution.py:81
  489.1 12.0 %fusion.20 = f32[512,3072]{1,0:T(8,128)} fusion(f32[384,3072]{1,0:T(8,128)S(1)} %bitcast.68, f32[512,384]{1,0:T(8,128)S(1)} %convolution_add_fusion), kind=kOutput, calls=%fused_computation.49 | convolution fusion | flops 7248543744 | bytes 11796480 | tf_op jit(solution)/shard_map/dot_general | solution.py:86
  501.4 136.0 %all-reduce.6.cloned.1.call-done = f32[512,3072]{1,0:T(8,128)} async-done(((f32[512,3072]{1,0:T(8,128)}), f32[512,3072]{1,0:T(8,128)}) %all-reduce.6.cloned.1.call-update) | async-done | bytes 6291472 | tf_op jit(solution)/shard_map/psum | solution.py:87
  637.3 9.5 %multiply_reduce_fusion.1 = (f32[]{:T(128)}, f32[512,3072]{1,0:T(8,128)S(1)}) fusion(f32[512,3072]{1,0:T(8,128)} %all-reduce.6.cloned.1.call-done, f32[512,3072]{1,0:T(8,128)} %all-reduce.4.cloned.1.call-done, f32[512,3072]{1,0:T(8,128)} %all-gather.23.cloned.1.call-done), kind=kLoop, calls=%fused_computation.16 | loop fusion | flops 6291455 | bytes 25165828 | tf_op jit(solution)/shard_map/reduce_sum | solution.py:89
  649.4 10.6 %fusion = f32[384,3072]{1,0:T(8,128)} fusion(f32[512,3072]{1,0:T(8,128)S(1)} %get-tuple-element.745, f32[512,384]{1,0:T(8,128)} %copy-done.2), kind=kOutput, calls=%fused_computation.20 | convolution fusion | flops 7250116608 | bytes 11796480 | tf_op jit(solution)/shard_map/dot_general | solution.py:91
  661.2 14.1 %multiply_reduce_fusion.3 = (f32[384]{0:T(512)S(1)}, f32[512,384]{1,0:T(8,128)S(1)}) fusion(f32[512]{0:T(512)S(1)} %get-tuple-element.757, f32[512,384]{1,0:T(8,128)S(1)} %copy-done.3, f32[384,3072]{1,0:T(8,128)} %param.21, f32[512,3072]{1,0:T(8,128)} %copy-done.1), kind=kOutput, calls=%fused_computation.44 | convolution fusion | flops 7251295744 | bytes 12586496 | tf_op jit(solution)/shard_map/dot_general | solution.py:98
  675.3 15.4 %fusion.26 = f32[3072,384]{1,0:T(8,128)} fusion(f32[512,384]{1,0:T(8,128)S(1)} %get-tuple-element.761, f32[512,3072]{1,0:T(8,128)} %all-reduce.4.cloned.1.call-done, f32[512,3072]{1,0:T(8,128)} %all-gather.23.cloned.1.call-done, f32[512]{0:T(512)S(1)} %get-tuple-element.757, f32[512]{0:T(512)S(1)} %get-tuple-element.756), kind=kOutput, calls=%fused_computation.76 | convolution fusion | flops 7252475904 | bytes 18092032 | tf_op jit(solution)/shard_map/dot_general | solution.py:106
  692.8 10.5 %all-reduce = (f32[384]{0:T(512)}, f32[]{:T(128)}) all-reduce(f32[384]{0:T(512)S(1)} %get-tuple-element.760, f32[]{:T(128)} %get-tuple-element.744), channel_id=1, replica_groups=mesh['row'=4,'col'=8] {'row'}, use_global_device_ids=true, to_apply=%region_26.0 | all-reduce | flops 385 | bytes 3080 | tf_op jit(solution)/shard_map/psum | solution.py:114
  703.9 13.4 %reduce-scatter.5.cloned.1.call-done = f32[384,768]{1,0:T(8,128)} async-done(((f32[384,3072]{1,0:T(8,128)}), f32[384,768]{1,0:T(8,128)}) %reduce-scatter.5.cloned.1.call-update) | async-done | bytes 1179664 | tf_op jit(solution)/shard_map/reduce_scatter | solution.py:112
  717.3 60.4 %reduce-scatter.3.cloned.1.call-done = f32[768,384]{1,0:T(8,128)} async-done(((f32[3072,384]{1,0:T(8,128)}), f32[768,384]{1,0:T(8,128)}) %reduce-scatter.3.cloned.1.call-update) | async-done | bytes 1179664 | tf_op jit(solution)/shard_map/reduce_scatter | solution.py:111
  (135 shorter events, 30.3 us)
Async XLA Ops:
  7.2 69.9 %all-gather.23.cloned.1.call-start = ((), (), s32[]{:S(2)}) async-start(), calls=%async_computation.2 | async-start | bytes 7077888 | tf_op jit(solution)/shard_map/all_gather | solution.py:45
  7.9 165.9 %all-gather.25.cloned.1.call-start = ((), (), s32[]{:S(2)}) async-start(), calls=%async_computation.3 | async-start | bytes 11796480 | tf_op jit(solution)/shard_map/all_gather | solution.py:46
  8.6 464.9 %all-reduce.4.cloned.1.call-start = ((), (), s32[]{:S(2)}) async-start(), calls=%async_computation.4 | async-start | bytes 12582912 | tf_op jit(solution)/shard_map/psum | solution.py:75
  173.8 5.5 copy-start
  266.7 73.1 %copy-start.5 = (f32[512]{0:T(512)}, f32[512]{0:T(512)S(1)}, u32[]{:S(2)}) copy-start(f32[512]{0:T(512)S(1)} %add_subtract_fusion.2) | copy-start | bytes 6148
  293.9 45.8 %copy-start.4 = (f32[768]{0:T(1024)}, f32[768]{0:T(1024)S(1)}, u32[]{:S(2)}) copy-start(f32[768]{0:T(1024)S(1)} %add_subtract_fusion) | copy-start | bytes 9220
  339.8 0.7 copy-start.6
  339.8 133.8 %copy-start.7 = (f32[384]{0:T(512)S(1)}, f32[384]{0:T(512)}, u32[]{:S(2)}) copy-start(f32[384]{0:T(512)} %param.20) | copy-start | bytes 4612
  339.8 149.3 %slice-start = ((s8[4718592]{0:T(1024)(128)(4,1)}), s8[524288]{0:T(1024)(128)(4,1)S(1)}, s32[]{:S(2)}) async-start(s8[4718592]{0:T(1024)(128)(4,1)} %bitcast.67), calls=%async_computation.8 | async-start | bytes 1048576
  339.8 297.5 %all-reduce.6.cloned.1.call-start = ((), (), s32[]{:S(2)}) async-start(), calls=%async_computation.5 | async-start | bytes 12582912 | tf_op jit(solution)/shard_map/psum | solution.py:87
  473.6 15.5 %slice-start.1 = ((s8[4718592]{0:T(1024)(128)(4,1)}), s8[4194304]{0:T(1024)(128)(4,1)S(1)}, s32[]{:S(2)}) async-start(s8[4718592]{0:T(1024)(128)(4,1)} %bitcast.67), calls=%async_computation.9 | async-start | bytes 8388608
  488.2 0.9 copy-start.2
  501.1 216.2 %reduce-scatter.5.cloned.1.call-start = ((), (), s32[]{:S(2)}) async-start(), calls=%async_computation.7 | async-start | bytes 5898240 | tf_op jit(solution)/shard_map/reduce_scatter | solution.py:112
  646.8 2.6 copy-start.1
  660.1 1.1 copy-start.3
  660.1 117.6 %reduce-scatter.3.cloned.1.call-start = ((), (), s32[]{:S(2)}) async-start(), calls=%async_computation.6 | async-start | bytes 5898240 | tf_op jit(solution)/shard_map/reduce_scatter | solution.py:111
Sparse Core Ops, SparseCore 0:
  9.6 67.4 all-gather.22
  78.9 94.8 all-gather.24
  339.9 133.6 all-reduce.3
  501.2 136.0 all-reduce.5
  660.2 57.0 reduce-scatter.4
  720.7 56.9 reduce-scatter.2
where the time goes:
time: 794 us; the launch traced here: 786 us
  waiting for transfers between devices  506 us (64%)
  blocking collectives  129 us (16%)
  matrix products  104 us (13%)
  other arithmetic  20.5 us (3%)
  between operations  16.6 us (2%)
  local copies, waits for them, and re-layouts  8.41 us (1%)
    psum x1, waiting for transfers between devices, body(): out = lax.psum(part_out, 'col')  136 us
    psum x1, waiting for transfers between devices, body(): whole_targets = lax.psum(partial_value, 'col')  133 us
    all_gather x10, blocking collectives, merged(): everything = jax.tree.map(lambda part: lax.all_gather(part, axis), array)  118 us
    all_gather x1, waiting for transfers between devices, body(): full_images = lax.all_gather(images, 'row', axis=1, tiled=True)  93.5 us
    all_gather x1, waiting for transfers between devices, body(): full_noise = lax.all_gather(noise, 'col', axis=1, tiled=True)  68.3 us
    reduce_scatter x1, waiting for transfers between devices, body(): lax.psum_scatter(local_in, 'row', scatter_dimension=0, tiled=True)  60.4 us
    dot_general x1, matrix products, body(): jnp.dot(weights, full_images, precision=highest, preferred_element_type=j...  19.3 us
    dot_general x1, matrix products, body(): lax.dot_general(full_noise, full_images, (((1,), (1,)), ((), ())), precis...  18.3 us
  transfers between devices with their start and end apart: 6, of which 6 were waited for; matrix products, arithmetic and copies ran while one was open for 4% of the time, Pallas kernels for 0%

commit v1 on v0

--- a/solution.py
+++ b/solution.py
@@ -42,7 +42,12 @@
 
 def body(noise, images, time_index, w_in, time_gain, w_out):
     highest = lax.Precision.HIGHEST
-    full_noise = lax.all_gather(noise, "col", axis=1, tiled=True)
+    ring = [noise]
+    for hop_ in range(7):
+        ring.append(lax.ppermute(ring[-1], "col", [(dev, (dev + 1) % 8) for dev in range(8)]))
+    full_noise = jnp.roll(
+        jnp.concatenate(ring[::-1], axis=1), (lax.axis_index("col") + 1) * ring[0].shape[1], axis=1
+    )
     full_images = lax.all_gather(images, "row", axis=1, tiled=True)
     width = full_noise.shape[1]
     noise_count = full_noise.shape[0] * lax.axis_size("row")

time: 794 us -> 728 us (0.917)
  waiting for transfers between devices: 506 us -> 436 us
  local copies, waits for them, and re-layouts: 8.41 us -> 19.8 us
  blocking collectives: 129 us -> 120 us
    ppermute x0 -> x7, waiting for transfers between devices: none -> 93.6 us  [body(): lax.ppermute(ring[-1], 'col', [(dev, (dev + 1) % 8) for dev in range(8)])]
    all_gather x1, waiting for transfers between devices: 93.5 us -> 0.02 us  [body(): full_images = lax.all_gather(images, 'row', axis=1, tiled=True)]
    all_gather x1 -> x0, waiting for transfers between devices: 68.3 us -> none  [body(): full_noise = lax.all_gather(noise, 'col', axis=1, tiled=True)]
    unnamed x34 -> x55, local copies, waits for them, and re-layouts: 5.92 us -> 17.2 us
    all_gather x10, blocking collectives: 118 us -> 109 us  [merged(): everything = jax.tree.map(lambda part: lax.all_gather(part, axis), array)]
  transfers between devices with their start and end apart: 6 -> 12, of which waited for: 6 -> 11; matrix products, arithmetic and copies ran while one was open for 4% -> 6% of each run, Pallas kernels for 0% -> 0%
where the time goes in v1:
time: 728 us; the launch traced here: 724 us
  waiting for transfers between devices  436 us (60%)
  blocking collectives  120 us (16%)
  matrix products  108 us (15%)
  other arithmetic  21.8 us (3%)
  local copies, waits for them, and re-layouts  19.8 us (3%)
  between operations  16.5 us (2%)
    psum x1, waiting for transfers between devices, body(): out = lax.psum(part_out, 'col')  136 us
    psum x1, waiting for transfers between devices, body(): whole_targets = lax.psum(partial_value, 'col')  133 us
    all_gather x10, blocking collectives, merged(): everything = jax.tree.map(lambda part: lax.all_gather(part, axis), array)  109 us
    ppermute x7, waiting for transfers between devices, body(): lax.ppermute(ring[-1], 'col', [(dev, (dev + 1) % 8) for dev in range(8)])  93.6 us
    reduce_scatter x1, waiting for transfers between devices, body(): lax.psum_scatter(local_in, 'row', scatter_dimension=0, tiled=True)  60.3 us
    dot_general x1, matrix products, body(): jnp.dot(weights, full_images, precision=highest, preferred_element_type=j...  19.3 us
    dot_general x1, matrix products, body(): lax.dot_general(full_noise, full_images, (((1,), (1,)), ((), ())), precis...  18.9 us
    dot_general x1, matrix products, body(): lax.dot_general(mixed, dpre, (((0,), (0,)), ((), ())), precision=highest,...  17.4 us
  transfers between devices with their start and end apart: 12, of which 11 were waited for; matrix products, arithmetic and copies ran while one was open for 6% of the time, Pallas kernels for 0%

profile of v1, /device:TPU:0, one launch (start us, length us, event | category | flops | bytes accessed | tf_op | source)
XLA Modules:
  0.0 723.7 jit_solution(12935812223855508904)
XLA Ops:
  8.5 13.9 %collective-permute-done = f32[512,384]{1,0:T(8,128)S(1)} collective-permute-done((f32[512,384]{1,0:T(8,128)}, f32[512,384]{1,0:T(8,128)S(1)}, u32[]{:S(2)}, u32[]{:S(2)}) %collective-permute-start) | collective-permute-done | bytes 786464 | tf_op jit(solution)/shard_map/ppermute | solution.py:47
  22.4 13.2 %collective-permute-done.1 = f32[512,384]{1,0:T(8,128)S(1)} collective-permute-done((f32[512,384]{1,0:T(8,128)S(1)}, f32[512,384]{1,0:T(8,128)S(1)}, u32[]{:S(2)}, u32[]{:S(2)}) %collective-permute-start.1) | collective-permute-done | bytes 786464 | tf_op jit(solution)/shard_map/ppermute | solution.py:47
  35.6 13.2 %collective-permute-done.2 = f32[512,384]{1,0:T(8,128)S(1)} collective-permute-done((f32[512,384]{1,0:T(8,128)S(1)}, f32[512,384]{1,0:T(8,128)S(1)}, u32[]{:S(2)}, u32[]{:S(2)}) %collective-permute-start.2) | collective-permute-done | bytes 786464 | tf_op jit(solution)/shard_map/ppermute | solution.py:47
  48.8 13.2 %collective-permute-done.3 = f32[512,384]{1,0:T(8,128)S(1)} collective-permute-done((f32[512,384]{1,0:T(8,128)S(1)}, f32[512,384]{1,0:T(8,128)S(1)}, u32[]{:S(2)}, u32[]{:S(2)}) %collective-permute-start.3) | collective-permute-done | bytes 786464 | tf_op jit(solution)/shard_map/ppermute | solution.py:47
  62.9 13.2 %collective-permute-done.4 = f32[512,384]{1,0:T(8,128)S(1)} collective-permute-done((f32[512,384]{1,0:T(8,128)S(1)}, f32[512,384]{1,0:T(8,128)S(1)}, u32[]{:S(2)}, u32[]{:S(2)}) %collective-permute-start.4) | collective-permute-done | bytes 786464 | tf_op jit(solution)/shard_map/ppermute | solution.py:47
  77.0 13.3 %collective-permute-done.5 = f32[512,384]{1,0:T(8,128)} collective-permute-done((f32[512,384]{1,0:T(8,128)S(1)}, f32[512,384]{1,0:T(8,128)}, u32[]{:S(2)}, u32[]{:S(2)}) %collective-permute-start.5) | collective-permute-done | bytes 786464 | tf_op jit(solution)/shard_map/ppermute | solution.py:47
  90.3 13.5 %collective-permute-done.6 = f32[512,384]{1,0:T(8,128)} collective-permute-done((f32[512,384]{1,0:T(8,128)}, f32[512,384]{1,0:T(8,128)}, u32[]{:S(2)}, u32[]{:S(2)}) %collective-permute-start.6) | collective-permute-done | bytes 786464 | tf_op jit(solution)/shard_map/ppermute | solution.py:47
  125.4 18.9 %subtract_reduce_fusion.3 = (f32[512]{0:T(512)S(1)}, f32[512,768]{1,0:T(8,128)S(1)}) fusion(f32[768,3072]{1,0:T(8,128)S(1)} %copy-done.1, f32[512,6144]{1,0:T(8,128)} %copy-done, s32[]{:T(128)S(6)} %select_n.72, f32[768]{0:T(1024)S(1)} %multiply_reduce_fusion, f32[512]{0:T(512)S(1)} %multiply_reduce_fusion.2), kind=kOutput, calls=%fused_computation.40 | convolution fusion | flops 14497873920 | bytes 17308676 | tf_op jit(solution)/shard_map/dot_general | solution.py:57
  144.7 12.8 %all-gather.11 = f32[8,1,512]{2,1,0:T(1,128)S(1)} all-gather(f32[1,1,512]{2,1,0:T(1,128)S(1)} %bitcast.94), channel_id=3, replica_groups=mesh['row'=4,'col'=8] {'col'}, dimensions={0}, use_global_device_ids=true | all-gather | bytes 18432 | tf_op jit(solution)/shard_map/all_gather | solution.py:12
  157.5 12.8 %all-gather.10 = f32[8,1,512]{2,1,0:T(1,128)S(1)} all-gather(f32[1,1,512]{2,1,0:T(1,128)S(1)} %bitcast.92), channel_id=2, replica_groups=mesh['row'=4,'col'=8] {'col'}, dimensions={0}, use_global_device_ids=true | all-gather | bytes 18432 | tf_op jit(solution)/shard_map/all_gather | solution.py:12
  188.9 12.8 %all-gather.15 = f32[8,1,512]{2,1,0:T(1,128)S(1)} all-gather(f32[1,1,512]{2,1,0:T(1,128)S(1)} %bitcast.93), channel_id=7, replica_groups=mesh['row'=4,'col'=8] {'col'}, dimensions={0}, use_global_device_ids=true | all-gather | bytes 18432 | tf_op jit(solution)/shard_map/all_gather | solution.py:12
  201.7 12.8 %all-gather.14 = f32[8,1,512]{2,1,0:T(1,128)S(1)} all-gather(f32[1,1,512]{2,1,0:T(1,128)S(1)} %bitcast.90), channel_id=6, replica_groups=mesh['row'=4,'col'=8] {'col'}, dimensions={0}, use_global_device_ids=true | all-gather | bytes 18432 | tf_op jit(solution)/shard_map/all_gather | solution.py:12
  231.9 12.8 %all-gather.19 = f32[8,1,512]{2,1,0:T(1,128)S(1)} all-gather(f32[1,1,512]{2,1,0:T(1,128)S(1)} %bitcast.95), channel_id=11, replica_groups=mesh['row'=4,'col'=8] {'col'}, dimensions={0}, use_global_device_ids=true | all-gather | bytes 18432 | tf_op jit(solution)/shard_map/all_gather | solution.py:12
  244.7 12.8 %all-gather.18 = f32[8,1,512]{2,1,0:T(1,128)S(1)} all-gather(f32[1,1,512]{2,1,0:T(1,128)S(1)} %bitcast.91), channel_id=10, replica_groups=mesh['row'=4,'col'=8] {'col'}, dimensions={0}, use_global_device_ids=true | all-gather | bytes 18432 | tf_op jit(solution)/shard_map/all_gather | solution.py:12
  257.8 19.3 %fusion.8 = f32[512,3072]{1,0:T(8,128)} fusion(f32[768,3072]{1,0:T(8,128)} %all-gather.22.cloned.1.call-done, f32[512,768]{1,0:T(8,128)S(1)} %get-tuple-element.759, f32[512]{0:T(512)S(1)} %log_add_fusion, f32[768]{0:T(1024)S(1)} %add_subtract_fusion), kind=kOutput, calls=%fused_computation.28 | convolution fusion | flops 14496301056 | bytes 17306624 | tf_op jit(solution)/shard_map/dot_general | solution.py:75
  277.8 133.1 %all-reduce.4.cloned.1.call-done = f32[512,3072]{1,0:T(8,128)} async-done(((f32[512,3072]{1,0:T(8,128)}), f32[512,3072]{1,0:T(8,128)}) %all-reduce.4.cloned.1.call-update) | async-done | bytes 6291472 | tf_op jit(solution)/shard_map/psum | solution.py:80
  411.0 15.1 %convolution_add_fusion = f32[512,384]{1,0:T(8,128)S(1)} fusion(f32[3072,384]{1,0:T(8,128)} %param.19, f32[384]{0:T(512)S(1)} %copy-done.9, f32[512]{0:T(512)S(1)} %get-tuple-element.757, f32[512,3072]{1,0:T(8,128)} %all-reduce.4.cloned.1.call-done, f32[512,6144]{1,0:T(8,128)} %copy-done, s32[]{:T(128)S(6)} %select_n.72, f32[512]{0:T(512)S(1)} %get-tuple-element.756), kind=kOutput, calls=%fused_computation.45 | convolution fusion | flops 7252869120 | bytes 18096132 | tf_op jit(solution)/shard_map/dot_general | solution.py:86
  426.1 12.1 %fusion.24 = f32[512,3072]{1,0:T(8,128)} fusion(f32[384,3072]{1,0:T(8,128)S(1)} %bitcast.67, f32[512,384]{1,0:T(8,128)S(1)} %convolution_add_fusion), kind=kOutput, calls=%fused_computation.51 | convolution fusion | flops 7248543744 | bytes 11796480 | tf_op jit(solution)/shard_map/dot_general | solution.py:91
  438.5 135.9 %all-reduce.6.cloned.1.call-done = f32[512,3072]{1,0:T(8,128)} async-done(((f32[512,3072]{1,0:T(8,128)}), f32[512,3072]{1,0:T(8,128)}) %all-reduce.6.cloned.1.call-update) | async-done | bytes 6291472 | tf_op jit(solution)/shard_map/psum | solution.py:92
  574.5 12.2 %multiply_reduce_fusion.1 = (f32[]{:T(128)}, f32[512,3072]{1,0:T(8,128)}) fusion(f32[512,3072]{1,0:T(8,128)} %all-reduce.6.cloned.1.call-done, f32[512,3072]{1,0:T(8,128)} %all-reduce.4.cloned.1.call-done, f32[512,6144]{1,0:T(8,128)} %copy-done, s32[]{:T(128)S(6)} %select_n.72), kind=kLoop, calls=%fused_computation.16 | loop fusion | flops 6291455 | bytes 25165832 | tf_op jit(solution)/shard_map/reduce_sum | solution.py:94
  598.1 14.1 %multiply_reduce_fusion.3 = (f32[384]{0:T(512)S(1)}, f32[512,384]{1,0:T(8,128)S(1)}) fusion(f32[512]{0:T(512)S(1)} %get-tuple-element.757, f32[512,384]{1,0:T(8,128)S(1)} %convolution_add_fusion, f32[384,3072]{1,0:T(8,128)} %param.21, f32[512,3072]{1,0:T(8,128)} %get-tuple-element.745), kind=kOutput, calls=%fused_computation.46 | convolution fusion | flops 7251295744 | bytes 12586496 | tf_op jit(solution)/shard_map/dot_general | solution.py:103
  612.1 17.4 %fusion.31 = f32[3072,384]{1,0:T(8,128)} fusion(f32[512,384]{1,0:T(8,128)S(1)} %get-tuple-element.761, f32[512,3072]{1,0:T(8,128)} %all-reduce.4.cloned.1.call-done, f32[512,6144]{1,0:T(8,128)} %copy-done, s32[]{:T(128)S(6)} %select_n.72, f32[512]{0:T(512)S(1)} %get-tuple-element.757, f32[512]{0:T(512)S(1)} %get-tuple-element.756), kind=kOutput, calls=%fused_computation.95 | convolution fusion | flops 7252475904 | bytes 18092036 | tf_op jit(solution)/shard_map/dot_general | solution.py:111
  643.2 12.0 %reduce-scatter.5.cloned.1.call-done = f32[384,768]{1,0:T(8,128)} async-done(((f32[384,3072]{1,0:T(8,128)}), f32[384,768]{1,0:T(8,128)}) %reduce-scatter.5.cloned.1.call-update) | async-done | bytes 1179664 | tf_op jit(solution)/shard_map/reduce_scatter | solution.py:117
  655.3 60.3 %reduce-scatter.3.cloned.1.call-done = f32[768,384]{1,0:T(8,128)} async-done(((f32[3072,384]{1,0:T(8,128)}), f32[768,384]{1,0:T(8,128)}) %reduce-scatter.3.cloned.1.call-update) | async-done | bytes 1179664 | tf_op jit(solution)/shard_map/reduce_scatter | solution.py:116
  (168 shorter events, 87.4 us)
Async XLA Ops:
  7.2 102.1 %copy-start.2 = (f32[512,384]{1,0:T(8,128)S(1)}, f32[512,384]{1,0:T(8,128)}, u32[]{:S(2)}) copy-start(f32[512,384]{1,0:T(8,128)} %param.16) | copy-start | bytes 2359300
  7.2 111.9 %all-gather.22.cloned.1.call-start = ((), (), s32[]{:S(2)}) async-start(), calls=%async_computation.2 | async-start | bytes 11796480 | tf_op jit(solution)/shard_map/all_gather | solution.py:51
  7.9 403.0 %all-reduce.4.cloned.1.call-start = ((), (), s32[]{:S(2)}) async-start(), calls=%async_computation.3 | async-start | bytes 12582912 | tf_op jit(solution)/shard_map/psum | solution.py:80
  8.0 14.5 %collective-permute-start = (f32[512,384]{1,0:T(8,128)}, f32[512,384]{1,0:T(8,128)S(1)}, u32[]{:S(2)}, u32[]{:S(2)}) collective-permute-start(f32[512,384]{1,0:T(8,128)} %param.16), channel_id=1, source_target_pairs={{0,1},{1,2},{2,3},{3,4},{4,5},{5,6},{6,7},{7,0},{8,9},{9,10},{10,1... | collective-permute-start | bytes 2359304 | tf_op jit(solution)/shard_map/ppermute | solution.py:47
  22.4 13.2 %collective-permute-start.1 = (f32[512,384]{1,0:T(8,128)S(1)}, f32[512,384]{1,0:T(8,128)S(1)}, u32[]{:S(2)}, u32[]{:S(2)}) collective-permute-start(f32[512,384]{1,0:T(8,128)S(1)} %collective-permute-done), channel_id=1, source_target_pairs={{0,1},{1,2},{2,3},{3,4},{4,5},{5,6},{6,7},{7,0},{8,9},{9,10},{10,1... | collective-permute-start | bytes 2359304 | tf_op jit(solution)/shard_map/ppermute | solution.py:47
  35.6 13.2 %collective-permute-start.2 = (f32[512,384]{1,0:T(8,128)S(1)}, f32[512,384]{1,0:T(8,128)S(1)}, u32[]{:S(2)}, u32[]{:S(2)}) collective-permute-start(f32[512,384]{1,0:T(8,128)S(1)} %collective-permute-done.1), channel_id=1, source_target_pairs={{0,1},{1,2},{2,3},{3,4},{4,5},{5,6},{6,7},{7,0},{8,9},{9,10},{10,1... | collective-permute-start | bytes 2359304 | tf_op jit(solution)/shard_map/ppermute | solution.py:47
  48.8 13.2 %collective-permute-start.3 = (f32[512,384]{1,0:T(8,128)S(1)}, f32[512,384]{1,0:T(8,128)S(1)}, u32[]{:S(2)}, u32[]{:S(2)}) collective-permute-start(f32[512,384]{1,0:T(8,128)S(1)} %collective-permute-done.2), channel_id=1, source_target_pairs={{0,1},{1,2},{2,3},{3,4},{4,5},{5,6},{6,7},{7,0},{8,9},{9,10},{10,1... | collective-permute-start | bytes 2359304 | tf_op jit(solution)/shard_map/ppermute | solution.py:47
  62.1 0.9 copy-start.3
  62.9 13.2 %collective-permute-start.4 = (f32[512,384]{1,0:T(8,128)S(1)}, f32[512,384]{1,0:T(8,128)S(1)}, u32[]{:S(2)}, u32[]{:S(2)}) collective-permute-start(f32[512,384]{1,0:T(8,128)S(1)} %collective-permute-done.3), channel_id=1, source_target_pairs={{0,1},{1,2},{2,3},{3,4},{4,5},{5,6},{6,7},{7,0},{8,9},{9,10},{10,1... | collective-permute-start | bytes 2359304 | tf_op jit(solution)/shard_map/ppermute | solution.py:47
  76.1 0.9 copy-start.5
  77.0 13.3 %collective-permute-start.5 = (f32[512,384]{1,0:T(8,128)S(1)}, f32[512,384]{1,0:T(8,128)}, u32[]{:S(2)}, u32[]{:S(2)}) collective-permute-start(f32[512,384]{1,0:T(8,128)S(1)} %collective-permute-done.4), channel_id=1, source_target_pairs={{0,1},{1,2},{2,3},{3,4},{4,5},{5,6},{6,7},{7,0},{8,9},{9,10},{10,1... | collective-permute-start | bytes 2359304 | tf_op jit(solution)/shard_map/ppermute | solution.py:47
  90.3 13.5 %collective-permute-start.6 = (f32[512,384]{1,0:T(8,128)}, f32[512,384]{1,0:T(8,128)}, u32[]{:S(2)}, u32[]{:S(2)}) collective-permute-start(f32[512,384]{1,0:T(8,128)} %collective-permute-done.5), channel_id=1, source_target_pairs={{0,1},{1,2},{2,3},{3,4},{4,5},{5,6},{6,7},{7,0},{8,9},{9,10},{10,1... | collective-permute-start | bytes 2359304 | tf_op jit(solution)/shard_map/ppermute | solution.py:47
  106.3 5.5 copy-start.6
  107.7 4.3 copy-start.4
  112.5 4.6 copy-start
  119.0 6.4 copy-start.1
  215.1 62.1 %copy-start.8 = (f32[512]{0:T(512)}, f32[512]{0:T(512)S(1)}, u32[]{:S(2)}) copy-start(f32[512]{0:T(512)S(1)} %add_subtract_fusion.2) | copy-start | bytes 6148
  231.2 45.9 %copy-start.7 = (f32[768]{0:T(1024)}, f32[768]{0:T(1024)S(1)}, u32[]{:S(2)}) copy-start(f32[768]{0:T(1024)S(1)} %add_subtract_fusion) | copy-start | bytes 9220
  277.1 133.8 %copy-start.9 = (f32[384]{0:T(512)S(1)}, f32[384]{0:T(512)}, u32[]{:S(2)}) copy-start(f32[384]{0:T(512)} %param.20) | copy-start | bytes 4612
  277.1 149.0 %slice-start = ((s8[4718592]{0:T(1024)(128)(4,1)}), s8[524288]{0:T(1024)(128)(4,1)S(1)}, s32[]{:S(2)}) async-start(s8[4718592]{0:T(1024)(128)(4,1)} %bitcast.66), calls=%async_computation.7 | async-start | bytes 1048576
  277.2 297.3 %all-reduce.6.cloned.1.call-start = ((), (), s32[]{:S(2)}) async-start(), calls=%async_computation.4 | async-start | bytes 12582912 | tf_op jit(solution)/shard_map/psum | solution.py:92
  411.0 15.2 %slice-start.1 = ((s8[4718592]{0:T(1024)(128)(4,1)}), s8[4194304]{0:T(1024)(128)(4,1)S(1)}, s32[]{:S(2)}) async-start(s8[4718592]{0:T(1024)(128)(4,1)} %bitcast.66), calls=%async_computation.8 | async-start | bytes 8388608
  438.2 217.0 %reduce-scatter.5.cloned.1.call-start = ((), (), s32[]{:S(2)}) async-start(), calls=%async_computation.6 | async-start | bytes 5898240 | tf_op jit(solution)/shard_map/reduce_scatter | solution.py:117
  598.0 117.6 %reduce-scatter.3.cloned.1.call-start = ((), (), s32[]{:S(2)}) async-start(), calls=%async_computation.5 | async-start | bytes 5898240 | tf_op jit(solution)/shard_map/reduce_scatter | solution.py:116
  (1 other events, 0.7 us)
Sparse Core Ops, SparseCore 0:
  9.8 98.9 all-gather.21
  277.3 133.6 all-reduce.3
  438.3 136.0 all-reduce.5
  598.1 57.0 reduce-scatter.4
  658.7 56.8 reduce-scatter.2
